TPU v7x, 512 devices: a whole 4x4x16 slice. The times are simulated.
512 devices in a mesh: mom: 8 (over y, x_lo), shard: 64 (over x_hi, z, core).
Axes of the slice: x: 4 (x_hi: 2, x_lo: 2; x = x_hi * 2 + x_lo), y: 4, z: 16, core: 2. Of those that a mesh axis runs over, the one named last changes fastest.
Arguments:
- green_ret: bfloat16 [8, 256, 8, 2, 128, 128], P('mom', 'shard'), may hold values from -4 to 4
- broadening: bfloat16 [2, 128, 128], replicated, may hold values from -0.5 to 0.5
- occupation: float32 [8, 256], P('mom', 'shard'), may hold values from 0.1 to 1
- neighbours: int32 [64, 4], replicated, may hold values from 0 to 63, as said below
- orbitals: int32 [64], replicated, may hold values from 4 to 16
- coupling: bfloat16 [64, 4, 256, 256], P('shard'), may hold values from -0.1875 to 0.1875
- phonon: float32 [8, 2, 256], replicated, may hold values from -5 to 5
- mode_table: int32 [8, 8], replicated, may hold values from 0 to 7, as said below
Outputs:
- self_energy: bfloat16 [8, 256, 64, 2, 256], P('mom', None, 'shard')
Inputs may be any that keep to these rules, and one draw needn't show every extreme that they name: `neighbours`: row a holds 4 distinct atoms of a's own layer block (atoms 8 * (a // 8) onward), none equal to a; the first is a with its lowest bit flipped. `mode_table`: each entry names one of the 8 phonon modes.
All inputs are finite; a program needn't handle non-finite values.
Results may differ from a plain program's by a relative error of at most 0.013.
Values may be sent and summed in bfloat16 or wider, within the bound.
No kernel may reach another device: no remote copies, remote signals or barrier semaphores. Data moves between devices by JAX's collectives and lax.ppermute only.
A program may use at most 192 MiB of HBM per device.

v0:
```python
import math
import jax
import jax.numpy as jnp
from jax import lax
from jax.sharding import PartitionSpec as P

NORB = 16
ATL = 8
NBR = 4
ENERGIES = 256
LAYERS = 8
PAIR = 256
ATOMS = 64


def dft_tables(length):
    counter = jnp.arange(length, dtype=jnp.int32)
    phases = counter[:, None] * counter[None, :] % length
    angles = phases.astype(jnp.float32) * (2.0 * math.pi / length)
    return (jnp.cos(angles).astype(jnp.bfloat16), jnp.sin(angles).astype(jnp.bfloat16))


def local(green_ret, broadening, occupation, neighbours, orbitals, coupling, phonon, mode_table):
    highest = lax.Precision.HIGHEST
    greens = green_ret[0]
    energy_dev = greens.shape[0]
    mixing = jnp.stack(
        [
            jnp.concatenate([broadening[0], broadening[1]], axis=1),
            jnp.concatenate([-broadening[1], broadening[0]], axis=1),
        ],
        axis=0,
    )
    left = jnp.einsum("elpik,pkq->eliq", greens, mixing, preferred_element_type=jnp.float32).astype(
        jnp.bfloat16
    )
    slot_atoms = neighbours % ATL
    selector = slot_atoms[:, :, None] == jnp.arange(ATL, dtype=jnp.int32)[None, None, :]
    layer_orbitals = jnp.repeat(orbitals.reshape(LAYERS, ATL), ATL, axis=0)
    partner_count = jnp.sum(jnp.where(selector, layer_orbitals[:, None, :], 0), axis=2)
    green_re = greens[:, :, 0]
    green_im = greens[:, :, 1]
    partner = jnp.stack(
        [
            jnp.concatenate([green_re, green_im], axis=-1),
            jnp.concatenate([-green_im, green_re], axis=-1),
        ],
        axis=2,
    )
    blocks = jnp.einsum("elik,elpjk->elpij", left, partner, preferred_element_type=jnp.float32)
    blocks = blocks.reshape(energy_dev, LAYERS, 2, ATL, NORB, ATL, NORB).transpose(
        0, 1, 3, 5, 2, 4, 6
    )
    slot_index = slot_atoms.reshape(LAYERS, ATL, NBR)
    chosen = jnp.take_along_axis(blocks, slot_index[None, :, :, :, None, None, None], axis=3)
    chosen = chosen.reshape(energy_dev, ATOMS, NBR, 2, NORB, NORB)
    counter = jnp.arange(NORB, dtype=jnp.int32)
    row_mask = counter[None, :] < orbitals[:, None]
    column_mask = counter[None, None, :] < partner_count[:, :, None]
    pair_mask = (row_mask[:, None, :, None] & column_mask[:, :, None, :]).astype(jnp.float32)
    scaled = (
        chosen * occupation[0][:, None, None, None, None, None] * pair_mask[None, :, :, None, :, :]
    )
    pair_blocks = scaled.reshape(energy_dev, ATOMS, NBR, 2, PAIR).astype(jnp.bfloat16)
    arrived = lax.all_to_all(pair_blocks, "shard", split_axis=1, concat_axis=0, tiled=True)
    atom_dev = arrived.shape[1]
    mixed_terms = jnp.einsum(
        "eanpx,anxy->eapy", arrived, coupling, preferred_element_type=jnp.float32
    )
    first_atom = lax.axis_index("shard") * atom_dev
    own_orbitals = lax.dynamic_slice_in_dim(orbitals, first_atom, atom_dev)
    pair_index = jnp.arange(PAIR, dtype=jnp.int32)
    own_mask = (
        (pair_index[None, :] // NORB < own_orbitals[:, None])
        & (pair_index[None, :] % NORB < own_orbitals[:, None])
    ).astype(jnp.float32)
    coupled = (mixed_terms * own_mask[None, :, None, :]).astype(jnp.bfloat16)
    cos_table, sin_table = dft_tables(ENERGIES)
    flat_coupled = coupled.reshape(ENERGIES, -1)
    part_cos = jnp.dot(cos_table, flat_coupled, preferred_element_type=jnp.float32).reshape(
        ENERGIES, atom_dev, 2, PAIR
    )
    part_sin = jnp.dot(sin_table, flat_coupled, preferred_element_type=jnp.float32).reshape(
        ENERGIES, atom_dev, 2, PAIR
    )
    time_data = jnp.stack(
        [part_cos[:, :, 0] + part_sin[:, :, 1], part_cos[:, :, 1] - part_sin[:, :, 0]], axis=2
    ).astype(jnp.bfloat16)
    own_momentum = lax.axis_index("mom")
    mode_count = phonon.shape[0]
    mode_ids = jnp.arange(mode_count, dtype=jnp.int32)
    own_modes = lax.dynamic_slice_in_dim(mode_table, own_momentum, 1, 0)[0]
    phonon_flat = phonon.reshape(mode_count, -1)
    received = lax.all_gather(time_data[None], "mom", axis=0, tiled=True)
    row_count = received.shape[0]
    one_hot = (own_modes[:, None] == mode_ids[None, :]).astype(jnp.float32)
    kernel = jnp.dot(one_hot, phonon_flat, precision=highest).reshape(row_count, 2, ENERGIES)
    values = received.astype(jnp.float32)
    kernel_re = kernel[:, 0][:, :, None, None]
    kernel_im = kernel[:, 1][:, :, None, None]
    add_re = jnp.sum(kernel_re * values[:, :, :, 0] - kernel_im * values[:, :, :, 1], axis=0)
    add_im = jnp.sum(kernel_re * values[:, :, :, 1] + kernel_im * values[:, :, :, 0], axis=0)
    summed = jnp.stack([add_re, add_im], axis=2)
    convolved = summed.astype(jnp.bfloat16)
    flat_conv = convolved.reshape(ENERGIES, -1)
    back_cos = jnp.dot(cos_table, flat_conv, preferred_element_type=jnp.float32).reshape(
        ENERGIES, atom_dev, 2, PAIR
    )
    back_sin = jnp.dot(sin_table, flat_conv, preferred_element_type=jnp.float32).reshape(
        ENERGIES, atom_dev, 2, PAIR
    )
    result_re = (back_cos[:, :, 0] - back_sin[:, :, 1]) * (1.0 / ENERGIES)
    result_im = (back_cos[:, :, 1] + back_sin[:, :, 0]) * (1.0 / ENERGIES)
    return jnp.stack([result_re, result_im], axis=2)[None].astype(jnp.bfloat16)


def solution(mesh):
    in_specs = (
        P("mom", "shard", None, None, None, None),
        P(),
        P("mom", "shard"),
        P(),
        P(),
        P("shard", None, None, None),
        P(),
        P(),
    )
    out_specs = P("mom", None, "shard", None, None)
    return jax.shard_map(local, mesh=mesh, in_specs=in_specs, out_specs=out_specs, check_vma=False)
```

profile of v0, /device:TPU:1, one launch (start us, length us, event | category | flops | bytes accessed | tf_op | source)
XLA Modules:
  0.0 248.5 jit_solution(2611192785870008069)
XLA Ops:
  6.5 1.8 copy.111
  8.3 1.1 slice_bitcast_fusion.2
  9.7 0.6 copy-done.1
  10.5 4.1 %maximum_bitcast_fusion = (bf16[4,8,1,128,256]{4,3,2,1,0:T(8,128)(2,1)}, bf16[4,8,1,128,256]{4,3,2,1,0:T(8,128)(2,1)}) fusion(bf16[4,8,128,128]{3,2,1,0:T(8,128)(2,1)S(1)} %get-tuple-element.9, bf16[4,8,128,128]{3,2,1,0:T(8,128)(2,1)} %get-tuple-element.10, bf16[4,8,128,128]{3,2,1,0:T(8,128)(2,1)S(1)} %fusion.75), kind=kLoop, calls=%fused_computation.9 | loop fusion | flops 8388608 | bytes 7340032 | tf_op jit(solution)/shard_map/stack | solution.py:43
  14.7 6.8 %fusion.4 = f32[4,8,2,128,128]{3,4,2,1,0:T(8,128)} fusion(bf16[4,8,1,128,256]{4,3,2,1,0:T(8,128)(2,1)} %get-tuple-element.16, bf16[4,8,1,128,256]{4,3,2,1,0:T(8,128)(2,1)} %get-tuple-element.15, bf16[1,4,8,2,128,128]{5,4,3,2,1,0:T(8,128)(2,1)} %param.8, bf16[1,128,256]{1,2,0:T(8,128)(2,1)S(1)} %get-tuple-element.20, ...), kind=kOutput, calls=%fused_computation.6 | convolution fusion | flops 1077149696 | bytes 10616832 | tf_op jit(solution)/shard_map/elik,elpjk->elpij/dot_general | solution.py:50
  21.5 19.6 %reshape.371 = f32[4,8,2,8,16,8,16]{4,3,6,5,2,1,0:T(8,128)} reshape(f32[4,8,2,128,128]{3,4,2,1,0:T(8,128)} %fusion.4) | data formatting | bytes 8388608 | tf_op jit(solution)/shard_map/reshape | solution.py:51
  41.1 33.9 %copy.72 = f32[4,8,2,8,16,8,16]{6,4,2,5,3,1,0:T(8,128)} copy(f32[4,8,2,8,16,8,16]{4,3,6,5,2,1,0:T(8,128)} %reshape.371) | data formatting | bytes 8388608 | tf_op jit(solution)/shard_map/reshape | solution.py:51
  75.1 14.9 %gather_fusion = f32[256,4,2,16,16]{4,3,2,1,0:T(8,128)} fusion(f32[4,8,8,8,2,16,16]{6,5,4,3,2,1,0:T(8,128)} %bitcast.180, s32[256]{0:T(256)S(1)} %reshape.378), kind=kCustom, calls=%fused_computation | custom fusion | bytes 4197376 | tf_op jit(solution)/shard_map/jit(take_along_axis)/gather | solution.py:55
  90.1 12.3 %reshape.392 = f32[4,64,4,2,256]{4,3,0,2,1:T(2,128)S(1)} reshape(f32[4,8,8,4,2,16,16]{6,5,4,0,3,2,1:T(8,128)} %bitcast.181) | data formatting | bytes 4194304 | tf_op jit(solution)/shard_map/jit(take_along_axis)/gather | solution.py:55
  103.1 1.6 fusion.10
  104.7 19.6 %all-to-all-start = ((bf16[4,64,4,2,256]{4,0,2,3,1:T(4,128)(2,1)}), bf16[4,64,4,2,256]{4,0,2,3,1:T(4,128)(2,1)S(1)}, u32[]{:S(2)}, u32[]{:S(2)}) async-start(bf16[4,64,4,2,256]{4,0,2,3,1:T(4,128)(2,1)} %fusion.10), calls=%async_computation | async-start | bytes 2097152 | tf_op jit(solution)/shard_map/all_to_all | solution.py:65
  124.4 0.6 dynamic_slice.7
  125.0 0.6 and_convert_fusion
  125.6 50.5 %all-to-all-done = bf16[4,64,4,2,256]{4,0,2,3,1:T(4,128)(2,1)S(1)} async-done(((bf16[4,64,4,2,256]{4,0,2,3,1:T(4,128)(2,1)}), bf16[4,64,4,2,256]{4,0,2,3,1:T(4,128)(2,1)S(1)}, u32[]{:S(2)}, u32[]{:S(2)}) %all-to-all-start) | async-done | bytes 1048608 | tf_op jit(solution)/shard_map/all_to_all | solution.py:65
  177.5 1.1 convolution_bitcast_fusion.2
  178.6 1.1 convolution_bitcast_fusion.3
  179.8 0.7 pad_maximum_fusion
  180.6 0.7 dynamic-slice_bitcast_fusion
  181.5 53.8 %all-gather.2.cloned.1.call-done = bf16[8,256,1,2,256]{4,1,3,2,0:T(8,128)(2,1)} async-done(((bf16[1,256,1,2,256]{4,1,3,2,0:T(8,128)(2,1)}), bf16[8,256,1,2,256]{4,1,3,2,0:T(8,128)(2,1)}) %all-gather.2.cloned.1.call-update) | async-done | bytes 2097168 | tf_op jit(solution)/shard_map/all_gather | solution.py:94
  235.3 2.0 convert_element_type.93
  237.3 0.8 subtract_reduce_fusion
  238.3 1.1 convolution_bitcast_fusion
  239.4 1.1 convolution_bitcast_fusion.1
  240.6 1.0 copy.83
  (44 shorter events, 3.3 us)
Async XLA Ops:
  6.5 170.4 %copy-start = (bf16[1,4,256,256]{3,2,1,0:T(8,128)(2,1)S(1)}, bf16[1,4,256,256]{3,2,1,0:T(8,128)(2,1)}, u32[]{:S(2)}) copy-start(bf16[1,4,256,256]{3,2,1,0:T(8,128)(2,1)} %param.13) | copy-start | bytes 1572868
  8.3 1.3 copy-start.2
  9.4 0.8 copy-start.1
  41.1 33.9 %copy-start.3 = (s32[64,4]{0,1:T(4,128)S(1)}, s32[64,4]{0,1:T(4,128)}, u32[]{:S(2)}) copy-start(s32[64,4]{0,1:T(4,128)} %param.11) | copy-start | bytes 3076
  90.1 13.0 %copy-start.4 = (f32[1,4]{1,0:T(1,128)S(1)}, f32[1,4]{1,0:T(1,128)}, u32[]{:S(2)}) copy-start(f32[1,4]{1,0:T(1,128)} %param.10) | copy-start | bytes 52
  104.7 71.4 %all-to-all-start = ((bf16[4,64,4,2,256]{4,0,2,3,1:T(4,128)(2,1)}), bf16[4,64,4,2,256]{4,0,2,3,1:T(4,128)(2,1)S(1)}, u32[]{:S(2)}, u32[]{:S(2)}) async-start(bf16[4,64,4,2,256]{4,0,2,3,1:T(4,128)(2,1)} %fusion.10), calls=%async_computation | async-start | bytes 2097152 | tf_op jit(solution)/shard_map/all_to_all | solution.py:65
  124.3 110.9 %all-gather.2.cloned.1.call-start = ((), (), s32[]{:S(2)}) async-start(), calls=%async_computation.1 | async-start | bytes 2359296 | tf_op jit(solution)/shard_map/all_gather | solution.py:94
  177.5 3.8 %copy-start.5 = (f32[8,2,256]{2,1,0:T(2,128)S(1)}, f32[8,2,256]{2,1,0:T(2,128)}, u32[]{:S(2)}) copy-start(f32[8,2,256]{2,1,0:T(2,128)} %param.14) | copy-start | bytes 49156
Sparse Core Ops, SparseCore 0:
  180.7 54.5 all-gather.1
where the time goes:
time: 250 us; the launch traced here: 248 us
  waiting for transfers between devices  104 us (42%)
  local copies, waits for them, and re-layouts  88.6 us (35%)
  starting transfers between devices  19.6 us (8%)
  between operations  13.6 us (5%)
  matrix products  11.9 us (5%)
  other arithmetic  10.5 us (4%)
    all_gather x1, waiting for transfers between devices, local(): received = lax.all_gather(time_data[None], 'mom', axis=0, tiled=True)  53.8 us
    reshape x2, local copies, waits for them, and re-layouts, local(): blocks.reshape(energy_dev, LAYERS, 2, ATL, NORB, ATL, NORB)  53.4 us
    all_to_all x1, waiting for transfers between devices, local(): lax.all_to_all(pair_blocks, 'shard', split_axis=1, concat_axis=0, tiled=T...  50.5 us
    gather x3, local copies, waits for them, and re-layouts, local(): jnp.take_along_axis(blocks, slot_index[None, :, :, :, None, None, None],...  27.4 us
    all_to_all x1, starting transfers between devices, local(): lax.all_to_all(pair_blocks, 'shard', split_axis=1, concat_axis=0, tiled=T...  19.6 us
    dot_general x1, matrix products, local(): jnp.einsum('elik,elpjk->elpij', left, partner, preferred_element_type=jnp...  6.77 us
  transfers between devices with their start and end apart: 2, of which 2 were waited for; matrix products, arithmetic and copies ran while one was open for 1% of the time, Pallas kernels for 0%

commit v1 on v0

--- a/solution.py
+++ b/solution.py
@@ -11,6 +11,13 @@
 LAYERS = 8
 PAIR = 256
 ATOMS = 64
+
+
+def point_matrix_by_axis(obj, dev_axis="mom"):
+    vec_out = jnp.stack([obj for _ in range(lax.psum(1, dev_axis))])
+    item_now = lax.all_to_all(vec_out, concat_axis=0, axis_name=dev_axis, split_axis=0)
+    carry_in = jnp.concatenate(item_now, axis=0)
+    return carry_in
 
 
 def dft_tables(length):
@@ -91,7 +98,7 @@
     mode_ids = jnp.arange(mode_count, dtype=jnp.int32)
     own_modes = lax.dynamic_slice_in_dim(mode_table, own_momentum, 1, 0)[0]
     phonon_flat = phonon.reshape(mode_count, -1)
-    received = lax.all_gather(time_data[None], "mom", axis=0, tiled=True)
+    received = point_matrix_by_axis(time_data[None])
     row_count = received.shape[0]
     one_hot = (own_modes[:, None] == mode_ids[None, :]).astype(jnp.float32)
     kernel = jnp.dot(one_hot, phonon_flat, precision=highest).reshape(row_count, 2, ENERGIES)

time: 250 us -> 214 us (0.86); the launches traced: 248 us -> 210 us
  waiting for transfers between devices: 104 us -> 75.6 us
  between operations: 13.6 us -> 0.22 us
  starting transfers between devices: 19.6 us -> 24.1 us
    all_gather x1 -> x0, waiting for transfers between devices: 53.8 us -> none  [local(): received = lax.all_gather(time_data[None], 'mom', axis=0, tiled=True)]
    all_to_all x0 -> x1, waiting for transfers between devices: none -> 25 us  [point_matrix_by_axis(): lax.all_to_all(vec_out, concat_axis=0, axis_name=dev_axis, split_axis=0)]
    all_to_all x0 -> x1, starting transfers between devices: none -> 4.36 us  [point_matrix_by_axis(): lax.all_to_all(vec_out, concat_axis=0, axis_name=dev_axis, split_axis=0)]
where the time goes in v1:
time: 214 us; the launch traced here: 210 us
  local copies, waits for them, and re-layouts  89.9 us (42%)
  waiting for transfers between devices  75.6 us (35%)
  starting transfers between devices  24.1 us (11%)
  matrix products  11.9 us (6%)
  other arithmetic  8.15 us (4%)
    reshape x2, local copies, waits for them, and re-layouts, local(): blocks.reshape(energy_dev, LAYERS, 2, ATL, NORB, ATL, NORB)  53.4 us
    all_to_all x1, waiting for transfers between devices, local(): lax.all_to_all(pair_blocks, 'shard', split_axis=1, concat_axis=0, tiled=T...  50.5 us
    gather x3, local copies, waits for them, and re-layouts, local(): jnp.take_along_axis(blocks, slot_index[None, :, :, :, None, None, None],...  27.4 us
    all_to_all x1, waiting for transfers between devices, point_matrix_by_axis(): lax.all_to_all(vec_out, concat_axis=0, axis_name=dev_axis, split_axis=0)  25 us
    all_to_all x1, starting transfers between devices, local(): lax.all_to_all(pair_blocks, 'shard', split_axis=1, concat_axis=0, tiled=T...  19.8 us
    dot_general x1, matrix products, local(): jnp.einsum('elik,elpjk->elpij', left, partner, preferred_element_type=jnp...  6.77 us
    all_to_all x1, starting transfers between devices, point_matrix_by_axis(): lax.all_to_all(vec_out, concat_axis=0, axis_name=dev_axis, split_axis=0)  4.36 us
  transfers between devices with their start and end apart: 2, of which 2 were waited for; matrix products, arithmetic and copies ran while one was open for 1% of the time, Pallas kernels for 0%

profile of v1, /device:TPU:1, one launch (start us, length us, event | category | flops | bytes accessed | tf_op | source)
XLA Modules:
  0.0 209.8 jit_solution(11283144335257559622)
XLA Ops:
  0.0 1.8 copy.129
  1.8 1.1 slice_bitcast_fusion.2
  3.1 0.6 copy-done.1
  4.0 4.1 %maximum_bitcast_fusion = (bf16[4,8,1,128,256]{4,3,2,1,0:T(8,128)(2,1)}, bf16[4,8,1,128,256]{4,3,2,1,0:T(8,128)(2,1)}) fusion(bf16[4,8,128,128]{3,2,1,0:T(8,128)(2,1)S(1)} %get-tuple-element.9, bf16[4,8,128,128]{3,2,1,0:T(8,128)(2,1)} %get-tuple-element.10, bf16[4,8,128,128]{3,2,1,0:T(8,128)(2,1)S(1)} %fusion.75), kind=kLoop, calls=%fused_computation.9 | loop fusion | flops 8388608 | bytes 7340032 | tf_op jit(solution)/shard_map/stack | solution.py:50
  8.1 6.8 %fusion.4 = f32[4,8,2,128,128]{3,4,2,1,0:T(8,128)} fusion(bf16[4,8,1,128,256]{4,3,2,1,0:T(8,128)(2,1)} %get-tuple-element.16, bf16[4,8,1,128,256]{4,3,2,1,0:T(8,128)(2,1)} %get-tuple-element.15, bf16[1,4,8,2,128,128]{5,4,3,2,1,0:T(8,128)(2,1)} %param.8, bf16[1,128,256]{1,2,0:T(8,128)(2,1)S(1)} %get-tuple-element.20, ...), kind=kOutput, calls=%fused_computation.6 | convolution fusion | flops 1077149696 | bytes 10616832 | tf_op jit(solution)/shard_map/elik,elpjk->elpij/dot_general | solution.py:57
  14.9 19.6 %reshape.378 = f32[4,8,2,8,16,8,16]{4,3,6,5,2,1,0:T(8,128)} reshape(f32[4,8,2,128,128]{3,4,2,1,0:T(8,128)} %fusion.4) | data formatting | bytes 8388608 | tf_op jit(solution)/shard_map/reshape | solution.py:58
  34.5 33.9 %copy.88 = f32[4,8,2,8,16,8,16]{6,4,2,5,3,1,0:T(8,128)} copy(f32[4,8,2,8,16,8,16]{4,3,6,5,2,1,0:T(8,128)} %reshape.378) | data formatting | bytes 8388608 | tf_op jit(solution)/shard_map/reshape | solution.py:58
  68.6 14.9 %gather_fusion = f32[256,4,2,16,16]{4,3,2,1,0:T(8,128)} fusion(f32[4,8,8,8,2,16,16]{6,5,4,3,2,1,0:T(8,128)} %bitcast.187, s32[256]{0:T(256)S(1)} %reshape.386), kind=kCustom, calls=%fused_computation | custom fusion | bytes 4197376 | tf_op jit(solution)/shard_map/jit(take_along_axis)/gather | solution.py:62
  83.5 12.3 %reshape.400 = f32[4,64,4,2,256]{4,3,0,2,1:T(2,128)S(1)} reshape(f32[4,8,8,4,2,16,16]{6,5,4,0,3,2,1:T(8,128)} %bitcast.188) | data formatting | bytes 4194304 | tf_op jit(solution)/shard_map/jit(take_along_axis)/gather | solution.py:62
  96.5 1.6 fusion.10
  98.2 19.8 %all-to-all-start = ((bf16[4,64,4,2,256]{4,0,2,3,1:T(4,128)(2,1)}), bf16[4,64,4,2,256]{4,0,2,3,1:T(4,128)(2,1)S(1)}, u32[]{:S(2)}, u32[]{:S(2)}) async-start(bf16[4,64,4,2,256]{4,0,2,3,1:T(4,128)(2,1)} %fusion.10), calls=%async_computation | async-start | bytes 2097152 | tf_op jit(solution)/shard_map/all_to_all | solution.py:72
  118.0 0.6 dynamic_slice.7
  118.5 0.6 and_convert_fusion
  119.2 50.5 %all-to-all-done = bf16[4,64,4,2,256]{4,0,2,3,1:T(4,128)(2,1)S(1)} async-done(((bf16[4,64,4,2,256]{4,0,2,3,1:T(4,128)(2,1)}), bf16[4,64,4,2,256]{4,0,2,3,1:T(4,128)(2,1)S(1)}, u32[]{:S(2)}, u32[]{:S(2)}) %all-to-all-start) | async-done | bytes 1048608 | tf_op jit(solution)/shard_map/all_to_all | solution.py:72
  170.9 1.1 convolution_bitcast_fusion.2
  172.0 1.1 convolution_bitcast_fusion.3
  173.3 1.5 stack.54
  174.8 4.4 %all-to-all-start.1 = ((bf16[8,1,256,1,2,256]{5,2,4,3,1,0:T(8,128)(2,1)}), bf16[8,1,256,1,2,256]{5,2,4,3,1,0:T(8,128)(2,1)S(1)}, u32[]{:S(2)}, u32[]{:S(2)}) async-start(bf16[8,1,256,1,2,256]{5,2,4,3,1,0:T(8,128)(2,1)} %stack.54), calls=%async_computation.1 | async-start | bytes 4194304 | tf_op jit(solution)/shard_map/all_to_all | solution.py:18
  179.2 0.7 dynamic-slice_bitcast_fusion
  180.1 25.0 %all-to-all-done.1 = bf16[8,1,256,1,2,256]{5,2,4,3,1,0:T(8,128)(2,1)S(1)} async-done(((bf16[8,1,256,1,2,256]{5,2,4,3,1,0:T(8,128)(2,1)}), bf16[8,1,256,1,2,256]{5,2,4,3,1,0:T(8,128)(2,1)S(1)}, u32[]{:S(2)}, u32[]{:S(2)}) %all-to-all-start.1) | async-done | bytes 2097184 | tf_op jit(solution)/shard_map/all_to_all | solution.py:18
  205.5 0.8 bitcast_reduce_fusion.1
  206.5 1.1 convolution_bitcast_fusion
  207.6 1.1 convolution_bitcast_fusion.1
  208.9 1.0 copy.101
  (44 shorter events, 3.5 us)
Async XLA Ops:
  0.0 170.4 %copy-start = (bf16[1,4,256,256]{3,2,1,0:T(8,128)(2,1)S(1)}, bf16[1,4,256,256]{3,2,1,0:T(8,128)(2,1)}, u32[]{:S(2)}) copy-start(bf16[1,4,256,256]{3,2,1,0:T(8,128)(2,1)} %param.13) | copy-start | bytes 1572868
  1.8 1.3 copy-start.2
  2.9 0.8 copy-start.1
  34.5 33.9 %copy-start.3 = (s32[64,4]{0,1:T(4,128)S(1)}, s32[64,4]{0,1:T(4,128)}, u32[]{:S(2)}) copy-start(s32[64,4]{0,1:T(4,128)} %param.11) | copy-start | bytes 3076
  83.5 13.0 %copy-start.4 = (f32[1,4]{1,0:T(1,128)S(1)}, f32[1,4]{1,0:T(1,128)}, u32[]{:S(2)}) copy-start(f32[1,4]{1,0:T(1,128)} %param.10) | copy-start | bytes 52
  98.2 71.6 %all-to-all-start = ((bf16[4,64,4,2,256]{4,0,2,3,1:T(4,128)(2,1)}), bf16[4,64,4,2,256]{4,0,2,3,1:T(4,128)(2,1)S(1)}, u32[]{:S(2)}, u32[]{:S(2)}) async-start(bf16[4,64,4,2,256]{4,0,2,3,1:T(4,128)(2,1)} %fusion.10), calls=%async_computation | async-start | bytes 2097152 | tf_op jit(solution)/shard_map/all_to_all | solution.py:72
  174.8 5.1 %copy-start.5 = (f32[8,2,256]{2,1,0:T(2,128)S(1)}, f32[8,2,256]{2,1,0:T(2,128)}, u32[]{:S(2)}) copy-start(f32[8,2,256]{2,1,0:T(2,128)} %param.14) | copy-start | bytes 49156
  174.8 30.3 %all-to-all-start.1 = ((bf16[8,1,256,1,2,256]{5,2,4,3,1,0:T(8,128)(2,1)}), bf16[8,1,256,1,2,256]{5,2,4,3,1,0:T(8,128)(2,1)S(1)}, u32[]{:S(2)}, u32[]{:S(2)}) async-start(bf16[8,1,256,1,2,256]{5,2,4,3,1,0:T(8,128)(2,1)} %stack.54), calls=%async_computation.1 | async-start | bytes 4194304 | tf_op jit(solution)/shard_map/all_to_all | solution.py:18
